TPU v7x, 256 devices: a whole 4x4x8 slice. The times are simulated.
256 devices in a mesh: seq: 8 (over z), head: 4 (over y_hi, core), rep: 8 (over y_lo, x).
Axes of the slice: x: 4, y: 4 (y_hi: 2, y_lo: 2; y = y_hi * 2 + y_lo), z: 8, core: 2. Of those that a mesh axis runs over, the one named last changes fastest.
Arguments:
- queries: bfloat16 [8, 2048, 7168], P('rep', 'seq', 'head'), may hold values from -6 to 6
- new_keys: bfloat16 [8, 2048, 7168], P('rep', 'seq', 'head'), may hold values from -6 to 6
- new_values: bfloat16 [8, 2048, 7168], P('rep', 'seq', 'head'), may hold values from -4 to 4
- lengths: int32 [8, 4], P('rep'), may hold values from 1 to 1024, 2048 in all within a row
- offsets: int32 [8, 4], P('rep'), may hold values from 0 to 4095
- slot_map: int32 [8, 4], P('rep'), may hold values from 0 to 3, each once within a row
Outputs:
- attended: bfloat16 [8, 2048, 7168], P('rep', 'seq', 'head')
- key_cache: bfloat16 [8, 4, 1024, 7168], P('rep', 'head', None, 'seq')
- value_cache: bfloat16 [8, 4, 1024, 7168], P('rep', 'head', None, 'seq')
Inputs may be any that keep to these rules, and one draw needn't show every extreme that they name: `lengths`: each row sums to 2048; its first entry is the group's shared prompt; every row has one entry equal to 1024. `slot_map`: each row is a permutation of the group's requests.
All inputs are finite; a program needn't handle non-finite values.
Results may differ from a plain program's by a relative error of at most 0.011.
Values may be sent and summed in bfloat16 or wider, within the bound.
A program may use at most 128 MiB of HBM per device.

v0:
```python
import math
import jax
import jax.numpy as jnp
from jax import lax
from jax.sharding import PartitionSpec as P

HD = 224
NEG_FILL = -1e30
ROPE_BASE = 10000.0
KEY_BLOCK = 512


def rotate(source, places):
    full_width = source.shape[-1]
    half_width = full_width // 2
    inverse = jnp.power(
        jnp.float32(ROPE_BASE), -2.0 * jnp.arange(half_width, dtype=jnp.float32) / full_width
    )
    angles = places.astype(jnp.float32)[:, None] * inverse[None, :]
    cosine = jnp.cos(angles)[:, None, :]
    sine_terms = jnp.sin(angles)[:, None, :]
    first_part = source[..., :half_width].astype(jnp.float32)
    second_part = source[..., half_width:].astype(jnp.float32)
    rotated = jnp.concatenate(
        [
            first_part * cosine - second_part * sine_terms,
            second_part * cosine + first_part * sine_terms,
        ],
        axis=-1,
    )
    return rotated.astype(jnp.bfloat16)


def token_request(token_ids, ends_at):
    return jnp.sum((token_ids[:, None] >= ends_at[None, :]).astype(jnp.int32), axis=1)


def lookup_rows(request, lookup):
    matches = request[:, None] == jnp.arange(lookup.shape[0], dtype=jnp.int32)[None, :]
    return jnp.sum(jnp.where(matches, lookup[None, :], 0), axis=1)


def empty_state(head_count, row_count):
    return (
        jnp.full((head_count, row_count), NEG_FILL, jnp.float32),
        jnp.zeros((head_count, row_count), jnp.float32),
        jnp.zeros((head_count, row_count, HD), jnp.float32),
    )


def finish(running):
    row_best, row_total, summed = running
    head_count, row_count, _ = summed.shape
    return (
        (summed / row_total[:, :, None])
        .transpose(1, 0, 2)
        .reshape(row_count, head_count * HD)
        .astype(jnp.bfloat16)
    )


def update(
    running, query_token_rows, query_tok, query_req, key_rows, value_rows, key_start, ends_at
):
    row_count = key_rows.shape[0]
    head_count = query_token_rows.shape[1]
    key_token_index = key_start + jnp.arange(row_count, dtype=jnp.int32)
    key_req = token_request(key_token_index, ends_at)
    same_request = (key_req[None, :] == query_req[:, None]) & (
        key_token_index[None, :] <= query_tok[:, None]
    )
    prompt_keys = (key_req[None, :] == 0) & (query_req[:, None] != 0)
    allowed = same_request | prompt_keys
    row_best, row_total, summed = running
    key_head_stack = key_rows.reshape(row_count, head_count, HD)
    value_heads = value_rows.reshape(row_count, head_count, HD)
    scores = jnp.einsum(
        "ezq,izq->zei", query_token_rows, key_head_stack, preferred_element_type=jnp.float32
    ) * (1.0 / math.sqrt(HD))
    scores = jnp.where(allowed[None], scores, NEG_FILL)
    best_new = jnp.maximum(row_best, jnp.max(scores, axis=2))
    factor = jnp.exp(row_best - best_new)
    weights = jnp.where(allowed[None], jnp.exp(scores - best_new[:, :, None]), 0.0)
    total_new = row_total * factor + jnp.sum(weights, axis=2)
    mixed = jnp.einsum(
        "eva,ael->evl",
        weights.astype(jnp.bfloat16),
        value_heads,
        preferred_element_type=jnp.float32,
    )
    return (best_new, total_new, summed * factor[:, :, None] + mixed)


def per_device(queries, new_keys, new_values, lengths, offsets, slot_map):
    tok_dev = queries.shape[1]
    local_cols = queries.shape[2]
    head_count = local_cols // HD
    tokens_total = tok_dev * lax.axis_size("seq")
    cache_len = tokens_total // 2
    lengths_row = lengths[0]
    offsets_row = offsets[0]
    slots_row = slot_map[0]
    request_count = lengths_row.shape[0]
    ends_at = jnp.cumsum(lengths_row)
    begins = ends_at - lengths_row
    token_ids = lax.axis_index("seq") * tok_dev + jnp.arange(tok_dev, dtype=jnp.int32)
    request = token_request(token_ids, ends_at)
    places = lookup_rows(request, offsets_row) + token_ids - lookup_rows(request, begins)
    rot_queries = rotate(queries[0].reshape(tok_dev, head_count, HD), places)
    rot_keys = rotate(new_keys[0].reshape(tok_dev, head_count, HD), places).reshape(
        tok_dev, local_cols
    )
    value_rows = new_values[0]
    key_rows = lax.all_gather(rot_keys, "seq", axis=0, tiled=True)
    piece_values = lax.all_gather(value_rows, "seq", axis=0, tiled=True)
    row_count = key_rows.shape[0]

    def key_step(key_index, state_in):
        first_row = key_index * KEY_BLOCK
        return update(
            state_in,
            rot_queries,
            token_ids,
            request,
            lax.dynamic_slice_in_dim(key_rows, first_row, KEY_BLOCK, 0),
            lax.dynamic_slice_in_dim(piece_values, first_row, KEY_BLOCK, 0),
            first_row,
            ends_at,
        )

    finished = lax.fori_loop(0, row_count // KEY_BLOCK, key_step, empty_state(head_count, tok_dev))
    attended = finish(finished)
    stacked = jnp.stack([rot_keys, value_rows])
    my_slot = lax.axis_index("head")
    request_ids = jnp.arange(request_count, dtype=jnp.int32)
    owner = jnp.sum(jnp.where(slots_row == my_slot, request_ids, 0))
    owner_begin = jnp.sum(jnp.where(request_ids == owner, begins, 0))
    slot_of = lookup_rows(request, slots_row)
    member = slot_of[None, :] == request_ids[:, None]
    buckets = jnp.where(member[None, :, :, None], stacked[:, None], jnp.zeros((), jnp.bfloat16))
    moved = lax.all_to_all(
        lax.all_to_all(buckets, "head", split_axis=1, concat_axis=3, tiled=True),
        "seq",
        split_axis=3,
        concat_axis=2,
        tiled=True,
    )
    padded = jnp.concatenate(
        [moved, jnp.zeros((2, 1, cache_len, moved.shape[3]), jnp.bfloat16)], axis=2
    )
    window = lax.dynamic_slice_in_dim(padded, owner_begin, cache_len, 2)
    return (attended[None], window[0:1], window[1:2])


def solution(mesh):
    in_specs = (
        P("rep", "seq", "head"),
        P("rep", "seq", "head"),
        P("rep", "seq", "head"),
        P("rep", None),
        P("rep", None),
        P("rep", None),
    )
    out_specs = (
        P("rep", "seq", "head"),
        P("rep", "head", None, "seq"),
        P("rep", "head", None, "seq"),
    )
    return jax.shard_map(
        per_device, mesh=mesh, in_specs=in_specs, out_specs=out_specs, check_vma=False
    )
```

profile of v0, /device:TPU:96, one launch (start us, length us, event | category | flops | bytes accessed | tf_op | source)
XLA Modules:
  0.0 385.8 jit_solution(3452643616625133445)
XLA Ops:
  8.8 1.5 copy.46
  14.9 1.4 pad_maximum_fusion
  16.3 2.8 copy.50
  19.1 3.4 broadcast_select_fusion
  22.6 5.6 %all-to-all-start = ((bf16[2,4,256,1792]{2,3,0,1:T(8,128)(2,1)}), bf16[2,4,256,1792]{2,3,0,1:T(8,128)(2,1)}, u32[]{:S(2)}, u32[]{:S(2)}) async-start(bf16[2,4,256,1792]{2,3,0,1:T(8,128)(2,1)} %broadcast_select_fusion), calls=%async_computation | async-start | bytes 14680064 | tf_op jit(solution)/shard_map/all_to_all | solution.py:142
  33.0 78.6 %all-to-all-done = bf16[2,4,256,1792]{2,3,0,1:T(8,128)(2,1)} async-done(((bf16[2,4,256,1792]{2,3,0,1:T(8,128)(2,1)}), bf16[2,4,256,1792]{2,3,0,1:T(8,128)(2,1)}, u32[]{:S(2)}, u32[]{:S(2)}) %all-to-all-start) | async-done | bytes 7340064 | tf_op jit(solution)/shard_map/all_to_all | solution.py:142
  111.6 3.6 copy.51
  115.2 47.2 %copy.52 = bf16[2,1,256,7168]{2,0,1,3:T(2,128)(2,1)} copy(bf16[2,1,256,7168]{2,3,0,1:T(8,128)(2,1)S(1)} %bitcast.73) | data formatting | bytes 14680064 | tf_op jit(solution)/shard_map/all_to_all | solution.py:142
  162.3 7.7 %all-to-all-start.1 = ((bf16[2,1,256,7168]{2,0,1,3:T(2,128)(2,1)}), bf16[2,1,256,7168]{2,0,1,3:T(2,128)(2,1)}, u32[]{:S(2)}, u32[]{:S(2)}) async-start(bf16[2,1,256,7168]{2,0,1,3:T(2,128)(2,1)} %copy.52), calls=%async_computation.1 | async-start | bytes 14680064 | tf_op jit(solution)/shard_map/all_to_all | solution.py:141
  170.0 106.1 %all-gather.6.cloned.1.call-done = bf16[1,2048,1792]{1,2,0:T(8,128)(2,1)} async-done(((bf16[1,256,1792]{1,2,0:T(8,128)(2,1)}), bf16[1,2048,1792]{1,2,0:T(8,128)(2,1)}) %all-gather.6.cloned.1.call-update) | async-done | bytes 7340048 | tf_op jit(solution)/shard_map/all_gather | solution.py:115
  276.2 51.9 %while.18 = (s32[]{:T(128)}, f32[8,256]{1,0:T(8,128)S(1)}, f32[8,256]{1,0:T(8,128)S(1)}, f32[8,256,224]{1,2,0:T(8,128)}, s32[4]{0:T(128)S(1)}, /*index=5*/s32[25...) while((s32[]{:T(128)}, f32[8,256]{1,0:T(8,128)S(1)}, ...), condition=%wide.region_8.9_spmd.clone, body=%wide.region_4.8_spmd.clone.sunk | while | flops 955204608 | bytes 45631228 | solution.py:131
  276.6 2.3 constant_dynamic-slice_fusion.3
  278.9 3.1 fusion.45
  281.9 3.3 fusion.46
  285.4 2.6 fusion.48
  288.4 2.3 constant_dynamic-slice_fusion.3
  290.7 3.1 fusion.45
  293.8 3.3 fusion.46
  297.2 4.1 %fusion.48 = f32[8,256,224]{1,2,0:T(8,128)} fusion(f32[8,256,224]{1,2,0:T(8,128)} %get-tuple-element.350, bf16[512,8,224]{0,2,1:T(8,128)(2,1)S(1)} %bitcast.71, f32[8,512,256]{2,1,0:T(8,128)S(1)} %copy-done, f32[8,256]{1,0:T(8,128)S(1)} %select_maximum_fusion.2, pred[256,512]{0,1:T(8,128)(4,1)S(1)} %and_or_fusion.2, ...), kind=kOutput, calls=%fused_computation.13.clone.1 | convolution fusion | flops 476381184 | bytes 9846785 | tf_op jit(solution)/shard_map/while/body/eval_jaxpr/eva,ael->evl/dot_general | solution.py:85
  301.8 2.3 constant_dynamic-slice_fusion.3
  304.1 3.1 fusion.45
  307.2 3.3 fusion.46
  310.6 4.1 %fusion.48 = f32[8,256,224]{1,2,0:T(8,128)} fusion(f32[8,256,224]{1,2,0:T(8,128)} %get-tuple-element.350, bf16[512,8,224]{0,2,1:T(8,128)(2,1)S(1)} %bitcast.71, f32[8,512,256]{2,1,0:T(8,128)S(1)} %copy-done, f32[8,256]{1,0:T(8,128)S(1)} %select_maximum_fusion.2, pred[256,512]{0,1:T(8,128)(4,1)S(1)} %and_or_fusion.2, ...), kind=kOutput, calls=%fused_computation.13.clone.1 | convolution fusion | flops 476381184 | bytes 9846785 | tf_op jit(solution)/shard_map/while/body/eval_jaxpr/eva,ael->evl/dot_general | solution.py:85
  315.1 2.3 constant_dynamic-slice_fusion.3
  317.4 3.1 fusion.45
  320.5 3.3 fusion.46
  323.9 4.1 %fusion.48 = f32[8,256,224]{1,2,0:T(8,128)} fusion(f32[8,256,224]{1,2,0:T(8,128)} %get-tuple-element.350, bf16[512,8,224]{0,2,1:T(8,128)(2,1)S(1)} %bitcast.71, f32[8,512,256]{2,1,0:T(8,128)S(1)} %copy-done, f32[8,256]{1,0:T(8,128)S(1)} %select_maximum_fusion.2, pred[256,512]{0,1:T(8,128)(4,1)S(1)} %and_or_fusion.2, ...), kind=kOutput, calls=%fused_computation.13.clone.1 | convolution fusion | flops 476381184 | bytes 9846785 | tf_op jit(solution)/shard_map/while/body/eval_jaxpr/eva,ael->evl/dot_general | solution.py:85
  328.1 1.6 divide_convert_fusion
  331.1 24.2 %all-to-all-done.1 = bf16[2,1,256,7168]{2,0,1,3:T(2,128)(2,1)} async-done(((bf16[2,1,256,7168]{2,0,1,3:T(2,128)(2,1)}), bf16[2,1,256,7168]{2,0,1,3:T(2,128)(2,1)}, u32[]{:S(2)}, u32[]{:S(2)}) %all-to-all-start.1) | async-done | bytes 7340064 | tf_op jit(solution)/shard_map/all_to_all | solution.py:141
  355.3 7.0 %copy.53 = bf16[2,1,256,7168]{2,3,0,1:T(8,128)(2,1)} copy(bf16[2,1,256,7168]{2,0,1,3:T(2,128)(2,1)} %all-to-all-done.1) | data formatting | bytes 14680064 | tf_op jit(solution)/shard_map/all_to_all | solution.py:141
  362.3 11.1 %copy.54 = bf16[2,1,8,256,896]{4,3,2,0,1:T(8,128)(2,1)} copy(bf16[2,1,8,256,896]{3,4,2,0,1:T(8,128)(2,1)} %bitcast.74) | data formatting | bytes 14680064 | tf_op jit(solution)/shard_map/all_to_all | solution.py:141
  373.4 5.6 %fusion.19 = (bf16[1,1,1024,896]{3,2,1,0:T(8,128)(2,1)}, bf16[1,1,1024,896]{3,2,1,0:T(8,128)(2,1)}) fusion(s32[]{:T(128)S(6)} %add.111, s32[]{:T(128)S(6)} %select_n.53, bf16[2,1,2048,896]{3,2,0,1:T(8,128)(2,1)} %bitcast.75), kind=kLoop, calls=%fused_computation.32 | loop fusion | bytes 11010056
  (81 shorter events, 12.4 us)
Async XLA Ops:
  7.2 5.8 %copy-start.2 = (bf16[1,256,1792]{2,1,0:T(8,128)(2,1)S(1)}, bf16[1,256,1792]{2,1,0:T(8,128)(2,1)}, u32[]{:S(2)}) copy-start(bf16[1,256,1792]{2,1,0:T(8,128)(2,1)} %param.10) | copy-start | bytes 2752516
  7.2 162.8 %all-gather.4.cloned.1.call-start = ((), (), s32[]{:S(2)}) async-start(), calls=%async_computation.2 | async-start | bytes 8257536 | tf_op jit(solution)/shard_map/all_gather | solution.py:114
  12.9 1.4 copy-start.1
  12.9 263.2 %all-gather.6.cloned.1.call-start = ((), (), s32[]{:S(2)}) async-start(), calls=%async_computation.3 | async-start | bytes 8257536 | tf_op jit(solution)/shard_map/all_gather | solution.py:115
  22.6 5.6 %copy-start.3 = (bf16[1,256,1792]{2,1,0:T(8,128)(2,1)S(1)}, bf16[1,256,1792]{2,1,0:T(8,128)(2,1)}, u32[]{:S(2)}) copy-start(bf16[1,256,1792]{2,1,0:T(8,128)(2,1)} %param.8) | copy-start | bytes 2752516
  22.6 6.2 %copy-start.5 = (s32[1,4]{1,0:T(1,128)S(1)}, s32[1,4]{1,0:T(1,128)}, u32[]{:S(2)}) copy-start(s32[1,4]{1,0:T(1,128)} %param.13) | copy-start | bytes 52
  22.6 6.9 %copy-start.4 = (s32[1,4]{1,0:T(1,128)S(1)}, s32[1,4]{1,0:T(1,128)}, u32[]{:S(2)}) copy-start(s32[1,4]{1,0:T(1,128)} %param.11) | copy-start | bytes 52
  22.6 89.0 %all-to-all-start = ((bf16[2,4,256,1792]{2,3,0,1:T(8,128)(2,1)}), bf16[2,4,256,1792]{2,3,0,1:T(8,128)(2,1)}, u32[]{:S(2)}, u32[]{:S(2)}) async-start(bf16[2,4,256,1792]{2,3,0,1:T(8,128)(2,1)} %broadcast_select_fusion), calls=%async_computation | async-start | bytes 14680064 | tf_op jit(solution)/shard_map/all_to_all | solution.py:142
  162.3 192.9 %all-to-all-start.1 = ((bf16[2,1,256,7168]{2,0,1,3:T(2,128)(2,1)}), bf16[2,1,256,7168]{2,0,1,3:T(2,128)(2,1)}, u32[]{:S(2)}, u32[]{:S(2)}) async-start(bf16[2,1,256,7168]{2,0,1,3:T(2,128)(2,1)} %copy.52), calls=%async_computation.1 | async-start | bytes 14680064 | tf_op jit(solution)/shard_map/all_to_all | solution.py:141
  281.9 3.4 copy-start
  293.8 3.4 copy-start
  307.1 3.4 copy-start
  320.5 3.4 copy-start
Sparse Core Ops, SparseCore 0:
  13.1 91.4 all-gather.3
  106.8 169.2 all-gather.5
where the time goes:
time: 387 us; the launch traced here: 386 us
  waiting for transfers between devices  209 us (54%)
  local copies, waits for them, and re-layouts  92 us (24%)
  other arithmetic  28 us (7%)
  matrix products  27.3 us (7%)
  between operations  16.1 us (4%)
  starting transfers between devices  13.3 us (3%)
    all_gather x1, waiting for transfers between devices, per_device(): piece_values = lax.all_gather(value_rows, 'seq', axis=0, tiled=True)  106 us
    all_to_all x1, waiting for transfers between devices, per_device(): lax.all_to_all(buckets, 'head', split_axis=1, concat_axis=3, tiled=True)  78.6 us
    all_to_all x2, local copies, waits for them, and re-layouts, per_device(): lax.all_to_all(buckets, 'head', split_axis=1, concat_axis=3, tiled=True)  50.7 us
    all_to_all x1, waiting for transfers between devices, per_device(): lax.all_to_all(lax.all_to_all(buckets, 'head', split_axis=1, concat_axis=...  24.2 us
    all_to_all x2, local copies, waits for them, and re-layouts, per_device(): lax.all_to_all(lax.all_to_all(buckets, 'head', split_axis=1, concat_axis=...  18.1 us
    dot_general x4, matrix products, update(): jnp.einsum('eva,ael->evl', weights.astype(jnp.bfloat16), value_heads, pre...  15 us
    reduce_sum x4, other arithmetic, update(): total_new = row_total * factor + jnp.sum(weights, axis=2)  13.3 us
    dot_general x4, matrix products, update(): jnp.einsum('ezq,izq->zei', query_token_rows, key_head_stack, preferred_el...  12.3 us
  transfers between devices with their start and end apart: 4, of which 3 were waited for; matrix products, arithmetic and copies ran while one was open for 31% of the time, Pallas kernels for 0%

commit v1 on v0

--- a/solution.py
+++ b/solution.py
@@ -112,7 +112,22 @@
     )
     value_rows = new_values[0]
     key_rows = lax.all_gather(rot_keys, "seq", axis=0, tiled=True)
-    piece_values = lax.all_gather(value_rows, "seq", axis=0, tiled=True)
+    ways, here, step = (lax.axis_size("seq"), lax.axis_index("seq"), value_rows.shape[0])
+    lengths_2 = [n * ways if d == 0 else n for d, n in enumerate(value_rows.shape)]
+    piece_values = lax.dynamic_update_slice_in_dim(
+        jnp.zeros(lengths_2, value_rows.dtype), value_rows, here * step, axis=0
+    )
+    going_up = going_down = value_rows
+    for far in range(1, ways // 2 + 1):
+        going_up = lax.ppermute(going_up, "seq", [(d, (d + 1) % ways) for d in range(ways)])
+        piece_values = lax.dynamic_update_slice_in_dim(
+            piece_values, going_up, (here - far) % ways * step, axis=0
+        )
+        if 2 * far < ways:
+            going_down = lax.ppermute(going_down, "seq", [(d, (d - 1) % ways) for d in range(ways)])
+            piece_values = lax.dynamic_update_slice_in_dim(
+                piece_values, going_down, (here + far) % ways * step, axis=0
+            )
     row_count = key_rows.shape[0]
 
     def key_step(key_index, state_in):

time: 387 us -> 432 us (1.12)
  the two profiles are of different devices: /device:TPU:96 before, /device:TPU:1 now
where the time goes in v1:
time: 432 us; the launch traced here: 431 us
  waiting for transfers between devices  225 us (52%)
  local copies, waits for them, and re-layouts  109 us (25%)
  other arithmetic  28.7 us (7%)
  matrix products  27.3 us (6%)
  starting transfers between devices  24.4 us (6%)
  between operations  16.2 us (4%)
    ppermute x4, waiting for transfers between devices, per_device(): lax.ppermute(going_up, 'seq', [(d, (d + 1) % ways) for d in range(ways)])  115 us
    all_to_all x1, waiting for transfers between devices, per_device(): lax.all_to_all(lax.all_to_all(buckets, 'head', split_axis=1, concat_axis=...  109 us
    all_to_all x2, local copies, waits for them, and re-layouts, per_device(): lax.all_to_all(buckets, 'head', split_axis=1, concat_axis=3, tiled=True)  50.7 us
    all_to_all x2, local copies, waits for them, and re-layouts, per_device(): lax.all_to_all(lax.all_to_all(buckets, 'head', split_axis=1, concat_axis=...  18.1 us
    dot_general x4, matrix products, update(): jnp.einsum('eva,ael->evl', weights.astype(jnp.bfloat16), value_heads, pre...  15 us
    reduce_sum x4, other arithmetic, update(): total_new = row_total * factor + jnp.sum(weights, axis=2)  13.3 us
    dot_general x4, matrix products, update(): jnp.einsum('ezq,izq->zei', query_token_rows, key_head_stack, preferred_el...  12.3 us
    unnamed x13, local copies, waits for them, and re-layouts  10.5 us
  transfers between devices with their start and end apart: 10, of which 5 were waited for; matrix products, arithmetic and copies ran while one was open for 31% of the time, Pallas kernels for 0%

profile of v1, /device:TPU:1, one launch (start us, length us, event | category | flops | bytes accessed | tf_op | source)
XLA Modules:
  0.0 430.5 jit_solution(17978324677844821165)
XLA Ops:
  15.8 2.8 copy.50
  18.6 3.4 broadcast_select_fusion
  22.0 8.8 %all-to-all-start = ((bf16[2,4,256,1792]{2,3,0,1:T(8,128)(2,1)}), bf16[2,4,256,1792]{2,3,0,1:T(8,128)(2,1)}, u32[]{:S(2)}, u32[]{:S(2)}) async-start(bf16[2,4,256,1792]{2,3,0,1:T(8,128)(2,1)} %broadcast_select_fusion), calls=%async_computation | async-start | bytes 14680064 | tf_op jit(solution)/shard_map/all_to_all | solution.py:157
  31.5 4.0 collective-permute-start.1
  35.5 35.9 %collective-permute-done = bf16[256,1792]{0,1:T(8,128)(2,1)} collective-permute-done((bf16[256,1792]{0,1:T(8,128)(2,1)S(1)}, bf16[256,1792]{0,1:T(8,128)(2,1)}, u32[]{:S(2)}, u32[]{:S(2)}) %collective-permute-start) | collective-permute-done | bytes 917536 | tf_op jit(solution)/shard_map/ppermute | solution.py:122
  73.8 2.7 collective-permute-start.3
  80.8 29.6 %collective-permute-done.2 = bf16[256,1792]{0,1:T(8,128)(2,1)} collective-permute-done((bf16[256,1792]{0,1:T(8,128)(2,1)}, bf16[256,1792]{0,1:T(8,128)(2,1)}, u32[]{:S(2)}, u32[]{:S(2)}) %collective-permute-start.2) | collective-permute-done | bytes 917536 | tf_op jit(solution)/shard_map/ppermute | solution.py:122
  111.7 3.9 broadcast_in_dim.165
  122.5 26.6 %collective-permute-done.4 = bf16[256,1792]{0,1:T(8,128)(2,1)S(1)} collective-permute-done((bf16[256,1792]{0,1:T(8,128)(2,1)}, bf16[256,1792]{0,1:T(8,128)(2,1)S(1)}, u32[]{:S(2)}, u32[]{:S(2)}) %collective-permute-start.4) | collective-permute-done | bytes 917536 | tf_op jit(solution)/shard_map/ppermute | solution.py:122
  155.7 23.3 %collective-permute-done.6 = bf16[256,1792]{0,1:T(8,128)(2,1)S(1)} collective-permute-done((bf16[256,1792]{0,1:T(8,128)(2,1)S(1)}, bf16[256,1792]{0,1:T(8,128)(2,1)S(1)}, u32[]{:S(2)}, u32[]{:S(2)}) %collective-permute-start.6) | collective-permute-done | bytes 917536 | tf_op jit(solution)/shard_map/ppermute | solution.py:122
  180.0 3.6 copy.51
  183.6 47.2 %copy.52 = bf16[2,1,256,7168]{2,0,1,3:T(2,128)(2,1)} copy(bf16[2,1,256,7168]{2,3,0,1:T(8,128)(2,1)S(1)} %bitcast.74) | data formatting | bytes 14680064 | tf_op jit(solution)/shard_map/all_to_all | solution.py:157
  230.7 5.0 %all-to-all-start.1 = ((bf16[2,1,256,7168]{2,0,1,3:T(2,128)(2,1)}), bf16[2,1,256,7168]{2,0,1,3:T(2,128)(2,1)}, u32[]{:S(2)}, u32[]{:S(2)}) async-start(bf16[2,1,256,7168]{2,0,1,3:T(2,128)(2,1)} %copy.52), calls=%async_computation.1 | async-start | bytes 14680064 | tf_op jit(solution)/shard_map/all_to_all | solution.py:156
  235.8 52.0 %while.18 = (s32[]{:T(128)}, f32[8,256]{1,0:T(8,128)S(1)}, f32[8,256]{1,0:T(8,128)S(1)}, f32[8,256,224]{1,2,0:T(8,128)}, s32[4]{0:T(128)S(1)}, /*index=5*/s32[25...) while((s32[]{:T(128)}, f32[8,256]{1,0:T(8,128)S(1)}, ...), condition=%wide.region_8.9_spmd.clone, body=%wide.region_4.8_spmd.clone.sunk | while | flops 955204608 | bytes 45631220 | solution.py:146
  236.2 2.3 constant_dynamic-slice_fusion.3
  238.5 3.1 fusion.45
  241.6 3.3 fusion.46
  245.0 2.6 fusion.48
  250.4 3.1 fusion.45
  253.4 3.3 fusion.46
  256.9 4.1 fusion.48
  261.4 2.3 constant_dynamic-slice_fusion.3
  263.7 3.1 fusion.45
  266.8 3.3 fusion.46
  270.3 4.1 fusion.48
  277.1 3.1 fusion.45
  280.2 3.3 fusion.46
  283.6 4.1 fusion.48
  290.8 109.2 %all-to-all-done.1 = bf16[2,1,256,7168]{2,0,1,3:T(2,128)(2,1)} async-done(((bf16[2,1,256,7168]{2,0,1,3:T(2,128)(2,1)}), bf16[2,1,256,7168]{2,0,1,3:T(2,128)(2,1)}, u32[]{:S(2)}, u32[]{:S(2)}) %all-to-all-start.1) | async-done | bytes 7340064 | tf_op jit(solution)/shard_map/all_to_all | solution.py:156
  400.0 7.0 %copy.53 = bf16[2,1,256,7168]{2,3,0,1:T(8,128)(2,1)} copy(bf16[2,1,256,7168]{2,0,1,3:T(2,128)(2,1)} %all-to-all-done.1) | data formatting | bytes 14680064 | tf_op jit(solution)/shard_map/all_to_all | solution.py:156
  407.0 11.1 %copy.54 = bf16[2,1,8,256,896]{4,3,2,0,1:T(8,128)(2,1)} copy(bf16[2,1,8,256,896]{3,4,2,0,1:T(8,128)(2,1)} %bitcast.75) | data formatting | bytes 14680064 | tf_op jit(solution)/shard_map/all_to_all | solution.py:156
  418.1 5.6 %fusion.19 = (bf16[1,1,1024,896]{3,2,1,0:T(8,128)(2,1)}, bf16[1,1,1024,896]{3,2,1,0:T(8,128)(2,1)}) fusion(s32[]{:T(128)S(6)} %add.188, s32[]{:T(128)S(6)} %select_n.123, bf16[2,1,2048,896]{3,2,0,1:T(8,128)(2,1)} %bitcast.76), kind=kLoop, calls=%fused_computation.32 | loop fusion | bytes 11010056
  (99 shorter events, 39.2 us)
Async XLA Ops:
  7.2 228.6 %all-gather.2.cloned.1.call-start = ((), (), s32[]{:S(2)}) async-start(), calls=%async_computation.2 | async-start | bytes 8257536 | tf_op jit(solution)/shard_map/all_gather | solution.py:114
  8.7 5.7 %copy-start.1 = (bf16[1,256,1792]{2,1,0:T(8,128)(2,1)S(1)}, bf16[1,256,1792]{2,1,0:T(8,128)(2,1)}, u32[]{:S(2)}) copy-start(bf16[1,256,1792]{2,1,0:T(8,128)(2,1)} %param.10) | copy-start | bytes 2752516
  22.0 50.8 %copy-start.4 = (s32[1,4]{1,0:T(1,128)S(1)}, s32[1,4]{1,0:T(1,128)}, u32[]{:S(2)}) copy-start(s32[1,4]{1,0:T(1,128)} %param.13) | copy-start | bytes 52
  22.0 157.9 %all-to-all-start = ((bf16[2,4,256,1792]{2,3,0,1:T(8,128)(2,1)}), bf16[2,4,256,1792]{2,3,0,1:T(8,128)(2,1)}, u32[]{:S(2)}, u32[]{:S(2)}) async-start(bf16[2,4,256,1792]{2,3,0,1:T(8,128)(2,1)} %broadcast_select_fusion), calls=%async_computation | async-start | bytes 14680064 | tf_op jit(solution)/shard_map/all_to_all | solution.py:157
  30.9 45.7 %copy-start.3 = (s32[1,4]{1,0:T(1,128)S(1)}, s32[1,4]{1,0:T(1,128)}, u32[]{:S(2)}) copy-start(s32[1,4]{1,0:T(1,128)} %param.11) | copy-start | bytes 52
  31.4 40.0 %collective-permute-start = (bf16[256,1792]{0,1:T(8,128)(2,1)S(1)}, bf16[256,1792]{0,1:T(8,128)(2,1)}, u32[]{:S(2)}, u32[]{:S(2)}) collective-permute-start(bf16[256,1792]{0,1:T(8,128)(2,1)S(1)} %bitcast.79), channel_id=1, source_target_pairs={{0,32},{32,64},{64,96},{96,128},{128,160},{160,192},{192,224},{224... | collective-permute-start | bytes 2752520 | tf_op jit(solution)/shard_map/ppermute | solution.py:122
  31.5 42.3 %collective-permute-start.1 = (bf16[256,1792]{0,1:T(8,128)(2,1)S(1)}, bf16[256,1792]{0,1:T(8,128)(2,1)}, u32[]{:S(2)}, u32[]{:S(2)}) collective-permute-start(bf16[256,1792]{0,1:T(8,128)(2,1)S(1)} %bitcast.80), channel_id=1, source_target_pairs={{0,224},{32,0},{64,32},{96,64},{128,96},{160,128},{192,160},{224,1... | collective-permute-start | bytes 2752520 | tf_op jit(solution)/shard_map/ppermute | solution.py:127
  71.4 39.1 %collective-permute-start.2 = (bf16[256,1792]{0,1:T(8,128)(2,1)}, bf16[256,1792]{0,1:T(8,128)(2,1)}, u32[]{:S(2)}, u32[]{:S(2)}) collective-permute-start(bf16[256,1792]{0,1:T(8,128)(2,1)} %collective-permute-done), channel_id=1, source_target_pairs={{0,32},{32,64},{64,96},{96,128},{128,160},{160,192},{192,224},{224... | collective-permute-start | bytes 2752520 | tf_op jit(solution)/shard_map/ppermute | solution.py:122
  73.8 45.0 %collective-permute-start.3 = (bf16[256,1792]{0,1:T(8,128)(2,1)}, bf16[256,1792]{0,1:T(8,128)(2,1)S(1)}, u32[]{:S(2)}, u32[]{:S(2)}) collective-permute-start(bf16[256,1792]{0,1:T(8,128)(2,1)} %collective-permute-done.1), channel_id=1, source_target_pairs={{0,224},{32,0},{64,32},{96,64},{128,96},{160,128},{192,160},{224,1... | collective-permute-start | bytes 2752520 | tf_op jit(solution)/shard_map/ppermute | solution.py:127
  110.4 38.7 %collective-permute-start.4 = (bf16[256,1792]{0,1:T(8,128)(2,1)}, bf16[256,1792]{0,1:T(8,128)(2,1)S(1)}, u32[]{:S(2)}, u32[]{:S(2)}) collective-permute-start(bf16[256,1792]{0,1:T(8,128)(2,1)} %collective-permute-done.2), channel_id=1, source_target_pairs={{0,32},{32,64},{64,96},{96,128},{128,160},{160,192},{192,224},{224... | collective-permute-start | bytes 2752520 | tf_op jit(solution)/shard_map/ppermute | solution.py:122
  118.8 35.8 %collective-permute-start.5 = (bf16[256,1792]{0,1:T(8,128)(2,1)S(1)}, bf16[256,1792]{0,1:T(8,128)(2,1)S(1)}, u32[]{:S(2)}, u32[]{:S(2)}) collective-permute-start(bf16[256,1792]{0,1:T(8,128)(2,1)S(1)} %collective-permute-done.3), channel_id=1, source_target_pairs={{0,224},{32,0},{64,32},{96,64},{128,96},{160,128},{192,160},{224,1... | collective-permute-start | bytes 2752520 | tf_op jit(solution)/shard_map/ppermute | solution.py:127
  149.1 29.8 %collective-permute-start.6 = (bf16[256,1792]{0,1:T(8,128)(2,1)S(1)}, bf16[256,1792]{0,1:T(8,128)(2,1)S(1)}, u32[]{:S(2)}, u32[]{:S(2)}) collective-permute-start(bf16[256,1792]{0,1:T(8,128)(2,1)S(1)} %collective-permute-done.4), channel_id=1, source_target_pairs={{0,32},{32,64},{64,96},{96,128},{128,160},{160,192},{192,224},{224... | collective-permute-start | bytes 2752520 | tf_op jit(solution)/shard_map/ppermute | solution.py:122
  230.7 5.0 %copy-start.2 = (bf16[256,8,224]{0,2,1:T(8,128)(2,1)S(1)}, bf16[256,8,224]{0,2,1:T(8,128)(2,1)}, u32[]{:S(2)}) copy-start(bf16[256,8,224]{0,2,1:T(8,128)(2,1)} %pad_maximum_fusion.1) | copy-start | bytes 2752516
  230.7 169.3 %all-to-all-start.1 = ((bf16[2,1,256,7168]{2,0,1,3:T(2,128)(2,1)}), bf16[2,1,256,7168]{2,0,1,3:T(2,128)(2,1)}, u32[]{:S(2)}, u32[]{:S(2)}) async-start(bf16[2,1,256,7168]{2,0,1,3:T(2,128)(2,1)} %copy.52), calls=%async_computation.1 | async-start | bytes 14680064 | tf_op jit(solution)/shard_map/all_to_all | solution.py:156
  241.6 3.4 copy-start
  253.4 3.4 copy-start
  266.8 3.4 copy-start
  280.2 3.4 copy-start
Sparse Core Ops, SparseCore 0:
  13.1 146.8 all-gather.1
